TPU v7x, 256 devices: a whole 4x4x8 slice. The times are simulated.
256 devices in a mesh: dp: 128 (over x, z, y_hi, core), shard: 2 (over y_lo).
Axes of the slice: x: 4, y: 4 (y_hi: 2, y_lo: 2; y = y_hi * 2 + y_lo), z: 8, core: 2. Of those that a mesh axis runs over, the one named last changes fastest.
Arguments:
- clips: bfloat16 [512, 5, 256, 512], P(('dp', 'shard')), may hold values from -16 to 16
- code_grad: bfloat16 [512, 5, 256, 18], P(('dp', 'shard')), may hold values from -6 to 6
- conv_weight: bfloat16 [1536, 512], replicated, may hold values from -0.15625 to 0.15625
- norm_gain: float32 [512], replicated, may hold values from 0.5 to 1.5
- proj_weight: bfloat16 [512, 18], replicated, may hold values from -0.25 to 0.25
- code_bias: float32 [18], replicated, may hold values from -1 to 1
- rotation: float32 [18, 18], replicated, may hold values from -1.5 to 1.5
- first_moment: float32 [1536, 512], P('shard'), may hold values from -4 to 4
- second_moment: float32 [1536, 512], P('shard'), may hold values from 0.01 to 0.3
Outputs:
- new_weight: bfloat16 [1536, 512], replicated
- first_moment_out: float32 [1536, 512], P('shard')
- second_moment_out: float32 [1536, 512], P('shard')
- input_grad: bfloat16 [512, 5, 256, 512], P(('dp', 'shard'))
- loss: float32 [], replicated
All inputs are finite; a program needn't handle non-finite values.
Results may differ from a plain program's by a relative error of at most 0.014.
Values may be sent and summed in bfloat16 or wider, within the bound.
No kernel may reach another device: no remote copies, remote signals or barrier semaphores. Data moves between devices by JAX's collectives and lax.ppermute only.
A program may use at most 128 MiB of HBM per device.

v0:
```python
import jax
import jax.numpy as jnp
from jax import lax
from jax.sharding import Mesh
from jax.sharding import PartitionSpec as P

DP = ("dp_0", "dp_1", "dp_2", "dp_3")
DP_SHARD = ("dp_0", "dp_1", "dp_2", "dp_3", "shard")


def one_axis_at_a_time(shard, axes):
    for axis in axes:
        shard = lax.psum(shard, axis)
    return shard


def split_up(shard, dim, count):
    before, after = (shard.shape[:dim], shard.shape[dim + 1 :])
    return jnp.moveaxis(shard.reshape(*before, count, -1, *after), dim, 0)


def sum_at_owner(shard, axis, dim):
    count = lax.axis_size(axis)
    tiles = lax.all_to_all(split_up(shard, dim, count), axis, 0, 0, tiled=True)
    return jnp.sum(tiles.astype(jnp.float32), axis=0)


def sum_at_owner_2(shard, axis, dim):
    count = lax.axis_size(axis)
    tiles = lax.all_to_all(split_up(shard, dim, count), axis, 0, 0, tiled=True)
    return jnp.sum(tiles, axis=0)


def sum_by_axis(shard, axes, dim):
    far, near = axes
    tiles = split_up(shard, dim, lax.axis_size(far))
    nearer = sum_at_owner_2(tiles, near, dim + 1)
    arrived = lax.all_to_all(nearer, far, split_axis=0, concat_axis=0, tiled=True)
    return arrived.sum(axis=0)


def filled_up(lines, count):
    spare = -len(lines) % count
    return jnp.pad(lines, [(0, spare)] + [(0, 0)] * (lines.ndim - 1))


def copy_for_each(shard, axis):
    copies = jnp.broadcast_to(shard, (lax.axis_size(axis), *shard.shape))
    return lax.all_to_all(copies, axis, split_axis=0, concat_axis=0, tiled=True)


def joined_along(tiles, dim):
    shape = list(tiles.shape[1:])
    shape[dim] *= tiles.shape[0]
    return jnp.moveaxis(tiles, 0, dim).reshape(shape)


def gathered_by_axis(shard, axes, dim):
    far, near = axes
    tiles = copy_for_each(copy_for_each(shard, far), near)
    return joined_along(tiles.swapaxes(0, 1).reshape(-1, *shard.shape), dim)


def total_of(shard, axes):
    lines = shard.reshape(-1, shard.shape[-1])
    own = sum_by_axis(filled_up(lines, lax.axis_size(axes[0]) * lax.axis_size(axes[1])), axes, 0)
    whole = gathered_by_axis(own, axes, 0)
    return whole[: len(lines)].reshape(shard.shape)


def collect(shard, axis, dim):
    tiles = copy_for_each(shard, axis)
    return joined_along(tiles, dim)


def stacked_taps(block):
    batch, frames, sites, width = block.shape
    padded = jnp.pad(block, ((0, 0), (2, 0), (0, 0), (0, 0)))
    taps = [padded[:, 2 - k : 2 - k + frames] for k in range(3)]
    return jnp.concatenate(taps, axis=3).reshape(batch * frames * sites, 3 * width)


def forward(block, conv_weight, norm_gain, proj_weight, code_bias, rotation):
    width = block.shape[3]
    stacked = stacked_taps(block)
    hidden = block.reshape(-1, width).astype(jnp.float32) + jnp.dot(
        stacked, conv_weight, preferred_element_type=jnp.float32
    )
    inverse = lax.rsqrt(jnp.mean(hidden * hidden, axis=1, keepdims=True) + 1e-06)
    unit = hidden * inverse
    normed = (unit * norm_gain).astype(jnp.bfloat16)
    latent = jnp.dot(normed, proj_weight, preferred_element_type=jnp.float32) + code_bias
    rotated = jnp.dot(latent, rotation, precision=lax.Precision.HIGHEST)
    codes = jnp.tanh(rotated)
    return (stacked, inverse, unit, rotated, codes)


def token_terms(rotated, codes, cotangent):
    probs = (1.0 + codes) / 2.0
    logit = 2.0 * rotated
    entropy = jax.nn.softplus(logit) - logit * probs
    token_loss = cotangent * codes + 0.25 * (rotated - codes) ** 2 + 0.1 * entropy
    return (probs, logit, jnp.sum(token_loss))


def backward(
    block, cotangent, conv_weight, norm_gain, proj_weight, rotation, saved, lean, clip_count
):
    stacked, inverse, unit, rotated, codes = saved
    probs = (1.0 + codes) / 2.0
    logit = 2.0 * rotated
    slope = 1.0 - codes * codes
    d_rot = (
        cotangent * slope
        + 0.5 * (rotated - codes) * (1.0 - slope)
        - 0.2 * logit * probs * (1.0 - probs)
        - 0.05 * slope * lean
    ) / clip_count
    d_lat = jnp.dot(d_rot, rotation.T, precision=lax.Precision.HIGHEST)
    d_norm = jnp.dot(d_lat, proj_weight.astype(jnp.float32).T, precision=lax.Precision.HIGHEST)
    scaled = d_norm * norm_gain
    d_hidden = inverse * (scaled - unit * jnp.mean(scaled * unit, axis=1, keepdims=True))
    d_conv = d_hidden.astype(jnp.bfloat16)
    batch, frames, sites, width = block.shape
    d_taps = lax.dot_general(
        d_conv, conv_weight, (((1,), (1,)), ((), ())), preferred_element_type=jnp.float32
    )
    d_taps = d_taps.reshape(batch, frames, sites, 3, width)
    padded = jnp.pad(d_taps, ((0, 0), (0, 2), (0, 0), (0, 0), (0, 0)))
    back = (
        padded[:, 0:frames, :, 0, :]
        + padded[:, 1 : frames + 1, :, 1, :]
        + padded[:, 2 : frames + 2, :, 2, :]
    )
    input_grad = (d_hidden.reshape(batch, frames, sites, width) + back).astype(jnp.bfloat16)
    return (stacked, d_conv, input_grad)


def on_device(
    clips,
    code_grad,
    conv_weight,
    norm_gain,
    proj_weight,
    code_bias,
    rotation,
    first_moment,
    second_moment,
):
    bit_count = code_grad.shape[3]
    devices = lax.axis_size(DP) * lax.axis_size("shard")
    clip_count = clips.shape[0] * devices
    token_count = clips.shape[0] * clips.shape[1] * clips.shape[2] * devices
    cotangent = code_grad.reshape(-1, bit_count).astype(jnp.float32)
    saved = forward(clips, conv_weight, norm_gain, proj_weight, code_bias, rotation)
    probs, logit, loss_part = token_terms(saved[3], saved[4], cotangent)
    bit_total, loss_total = (
        one_axis_at_a_time(jnp.sum(probs, axis=0), DP_SHARD),
        one_axis_at_a_time(loss_part, DP_SHARD),
    )
    bit_mean = bit_total / token_count
    code_entropy = jnp.sum(
        -bit_mean * jnp.log(bit_mean) - (1.0 - bit_mean) * jnp.log(1.0 - bit_mean)
    )
    loss = loss_total / token_count - 0.1 * code_entropy
    lean = jnp.log((1.0 - bit_mean) / bit_mean)
    stacked, d_conv, input_grad = backward(
        clips, cotangent, conv_weight, norm_gain, proj_weight, rotation, saved, lean, clip_count
    )
    owned_rows = first_moment.shape[0]
    group_part = sum_at_owner(
        lax.dot_general(
            stacked, d_conv, (((0,), (0,)), ((), ())), preferred_element_type=jnp.float32
        ).astype(jnp.bfloat16),
        "shard",
        0,
    )
    grad_owned = total_of(group_part, (("dp_0", "dp_1", "dp_2"), "dp_3"))
    first_out = 0.9 * first_moment + 0.1 * grad_owned
    second_out = 0.99 * second_moment + 0.01 * grad_owned * grad_owned
    owner = lax.axis_index("shard")
    own_weight = lax.dynamic_slice_in_dim(conv_weight, owner * owned_rows, owned_rows, 0).astype(
        jnp.float32
    )
    stepped = (own_weight - 0.001 * first_out / (jnp.sqrt(second_out) + 1e-08)).astype(jnp.bfloat16)
    new_weight = collect(stepped, "shard", 0)
    return (new_weight, first_out, second_out, input_grad, loss)


def solution(mesh):
    finer = Mesh(
        mesh.devices.reshape(4, 8, 2, 2, mesh.shape["shard"]),
        ("dp_0", "dp_1", "dp_2", "dp_3", "shard"),
    )
    in_specs = (
        P(DP_SHARD, None, None, None),
        P(DP_SHARD, None, None, None),
        P(),
        P(),
        P(),
        P(),
        P(),
        P("shard", None),
        P("shard", None),
    )
    out_specs = (P(), P("shard", None), P("shard", None), P(DP_SHARD, None, None, None), P())
    return jax.shard_map(
        on_device, mesh=finer, in_specs=in_specs, out_specs=out_specs, check_vma=False
    )
```

profile of v0, /device:TPU:1, one launch (start us, length us, event | category | flops | bytes accessed | tf_op | source)
XLA Modules:
  0.0 238.2 jit_solution(2002389347079798934)
XLA Ops:
  1.7 2.7 %pad_slice_fusion.3 = (bf16[2,5,256,512]{3,2,1,0:T(8,128)(2,1)S(1)}, bf16[2,5,256,512]{3,2,1,0:T(8,128)(2,1)S(1)}) fusion(bf16[2,5,256,512]{3,2,1,0:T(8,128)(2,1)} %param.9), kind=kLoop, calls=%fused_computation.14 | loop fusion | bytes 7864320 | tf_op jit(solution)/shard_map/slice | solution.py:79
  5.9 4.6 %multiply_reduce_fusion.1 = (f32[2560]{0:T(1024)S(1)}, f32[2560,512]{1,0:T(8,128)S(1)}) fusion(bf16[2560,1536]{1,0:T(8,128)(2,1)S(1)} %bitcast.29, bf16[1536,512]{1,0:T(8,128)(2,1)S(1)} %copy-done.6, bf16[2560,512]{1,0:T(8,128)(2,1)S(1)} %bitcast.27), kind=kOutput, calls=%fused_computation.11 | convolution fusion | flops 4031772160 | bytes 17311744 | tf_op jit(solution)/shard_map/dot_general | solution.py:86
  14.1 9.9 %all-reduce.3 = (f32[18]{0:T(128)S(1)}, f32[]{:T(128)}) all-reduce(f32[18]{0:T(128)S(1)} %get-tuple-element.6, f32[]{:T(128)} %get-tuple-element.5), channel_id=1, replica_groups=mesh['dp_0'=4,'dp_1'=8,'dp_2'=2,'dp_3'=2,'shard'=2] {'dp_0'}, use_global_device_ids=true, to_apply=%region_2.3 | all-reduce | flops 19 | bytes 152 | tf_op jit(solution)/shard_map/psum | solution.py:13
  24.0 16.9 %all-reduce.2 = (f32[18]{0:T(128)S(1)}, f32[]{:T(128)}) all-reduce(f32[18]{0:T(128)S(1)} %get-tuple-element.9, f32[]{:T(128)} %get-tuple-element.10), channel_id=1, replica_groups=mesh['dp_0'=4,'dp_1'=8,'dp_2'=2,'dp_3'=2,'shard'=2] {'dp_1'}, use_global_device_ids=true, to_apply=%region_3.4 | all-reduce | flops 19 | bytes 152 | tf_op jit(solution)/shard_map/psum | solution.py:13
  40.9 5.9 %all-reduce.6 = (f32[18]{0:T(128)S(1)}, f32[]{:T(128)}) all-reduce(f32[18]{0:T(128)S(1)} %get-tuple-element.7, f32[]{:T(128)} %get-tuple-element.8), channel_id=1, replica_groups=mesh['dp_0'=4,'dp_1'=8,'dp_2'=2,'dp_3'=2,'shard'=2] {'dp_2'}, use_global_device_ids=true, to_apply=%region_4.5 | all-reduce | flops 19 | bytes 152 | tf_op jit(solution)/shard_map/psum | solution.py:13
  46.8 10.3 %all-reduce.5 = (f32[18]{0:T(128)S(1)}, f32[]{:T(128)}) all-reduce(f32[18]{0:T(128)S(1)} %get-tuple-element.15, f32[]{:T(128)} %get-tuple-element.16), channel_id=1, replica_groups=mesh['dp_0'=4,'dp_1'=8,'dp_2'=2,'dp_3'=2,'shard'=2] {'dp_3'}, use_global_device_ids=true, to_apply=%region_5.6 | all-reduce | flops 19 | bytes 152 | tf_op jit(solution)/shard_map/psum | solution.py:13
  57.1 4.6 %all-reduce.4 = (f32[18]{0:T(128)S(1)}, f32[]{:T(128)}) all-reduce(f32[18]{0:T(128)S(1)} %get-tuple-element.13, f32[]{:T(128)} %get-tuple-element.14), channel_id=1, replica_groups=mesh['dp_0'=4,'dp_1'=8,'dp_2'=2,'dp_3'=2,'shard'=2] {'shard'}, use_global_device_ids=true, to_apply=%region_6.7 | all-reduce | flops 19 | bytes 152 | tf_op jit(solution)/shard_map/psum | solution.py:13
  62.9 5.8 %multiply_reduce_fusion = (f32[2560]{0:T(1024)S(1)}, f32[2560,512]{1,0:T(8,128)S(1)}) fusion(f32[2560,512]{1,0:T(8,128)} %copy-done.3, f32[2560]{0:T(1024)S(1)} %add_rsqrt_fusion, f32[512]{0:T(512)S(1)} %copy-done.8, f32[2560,18]{0,1:T(8,128)S(1)} %fusion.20, bf16[512,18]{0,1:T(8,128)(2,1)S(1)} %copy-done), kind=kOutput, calls=%fused_computation.9 | convolution fusion | flops 288355840 | bytes 10711040 | tf_op jit(solution)/shard_map/dot_general | solution.py:120
  68.7 1.6 subtract_multiply_fusion
  70.8 4.3 %convolution_convert_fusion = bf16[1536,512]{1,0:T(8,128)(2,1)S(1)} fusion(bf16[2560,1536]{1,0:T(8,128)(2,1)S(1)} %bitcast.32, f32[2560,512]{1,0:T(8,128)S(1)} %subtract_multiply_fusion), kind=kOutput, calls=%fused_computation.17 | convolution fusion | flops 4028628992 | bytes 14680064 | tf_op jit(solution)/shard_map/dot_general | solution.py:172
  75.1 20.2 %all_to_all.30 = bf16[2,768,512]{2,1,0:T(8,128)(2,1)S(1)} all-to-all(bf16[2,768,512]{2,1,0:T(8,128)(2,1)S(1)} %bitcast.35), channel_id=1, replica_groups=mesh['dp_0'=4,'dp_1'=8,'dp_2'=2,'dp_3'=2,'shard'=2] {'shard'}, dimensions={0} | all-to-all | bytes 3145728 | tf_op jit(solution)/shard_map/all_to_all | solution.py:24
  95.2 1.5 convert_reduce_fusion
  96.7 1.5 reshape_reshape.6
  99.1 7.1 %all_to_all.31 = f32[2,64,6,512]{3,1,2,0:T(8,128)S(1)} all-to-all(f32[2,64,6,512]{3,1,2,0:T(8,128)S(1)} %copy.26), channel_id=1, replica_groups=mesh['dp_0'=4,'dp_1'=8,'dp_2'=2,'dp_3'=2,'shard'=2] {'dp_3'}, dimensions={0} | all-to-all | bytes 3145728 | tf_op jit(solution)/shard_map/all_to_all | solution.py:30
  106.9 36.2 %all_to_all.32 = f32[64,6,512]{2,1,0:T(8,128)S(1)} all-to-all(f32[64,6,512]{2,1,0:T(8,128)S(1)} %copy.27), channel_id=1, replica_groups=mesh['dp_0'=4,'dp_1'=8,'dp_2'=2,'dp_3'=2,'shard'=2] {'dp_0','dp_1','dp_2'}, dimensions={0} | all-to-all | bytes 1572864 | tf_op jit(solution)/shard_map/all_to_all | solution.py:38
  144.3 6.9 %all-to-all-start.3 = ((f32[64,6,512]{2,1,0:T(8,128)}), f32[64,6,512]{2,1,0:T(8,128)S(1)}, u32[]{:S(2)}, u32[]{:S(2)}) async-start(f32[64,6,512]{2,1,0:T(8,128)} %broadcast_in_dim.6), calls=%async_computation.3 | async-start | bytes 2097152 | tf_op jit(solution)/shard_map/all_to_all | solution.py:49
  151.3 10.3 %fusion.6 = f32[2560,1536]{1,0:T(8,128)} fusion(bf16[1536,512]{1,0:T(8,128)(2,1)S(1)} %copy-done.7, f32[2560,512]{1,0:T(8,128)} %copy-done.2), kind=kOutput, calls=%fused_computation.24 | convolution fusion | flops 4027842560 | bytes 22544384 | tf_op jit(solution)/shard_map/dot_general | solution.py:125
  161.5 26.1 %reshape.52 = f32[2,5,256,3,512]{4,3,2,1,0:T(4,128)} reshape(f32[2560,1536]{1,0:T(8,128)} %fusion.6) | data formatting | bytes 31457280 | tf_op jit(solution)/shard_map/reshape | solution.py:128
  188.3 6.0 %all_to_all.33 = f32[2,64,6,512]{3,1,2,0:T(8,128)S(1)} all-to-all(f32[2,64,6,512]{3,1,2,0:T(8,128)S(1)} %broadcast_in_dim.7), channel_id=1, replica_groups=mesh['dp_0'=4,'dp_1'=8,'dp_2'=2,'dp_3'=2,'shard'=2] {'dp_3'}, dimensions={0} | all-to-all | bytes 3145728 | tf_op jit(solution)/shard_map/all_to_all | solution.py:49
  195.2 1.4 reshape_reshape.7
  196.6 5.3 %subtract_convert_fusion = (bf16[768,512]{1,0:T(8,128)(2,1)S(1)}, f32[768,512]{1,0:T(8,128)}, f32[768,512]{1,0:T(8,128)}) fusion(bf16[1536,512]{1,0:T(8,128)(2,1)} %param.11, s32[]{:T(128)S(6)} %select_n.7, f32[768,512]{1,0:T(8,128)} %reshape_reshape.7, f32[768,512]{1,0:T(8,128)} %param.16, f32[768,512]{1,0:T(8,128)} %param.17), kind=kLoop, calls=%fused_computation.22 | loop fusion | flops 5111808 | bytes 9437188 | tf_op jit(solution)/shard_map/convert_element_type | solution.py:185
  203.1 3.7 %all-to-all-start.5 = ((bf16[2,768,512]{2,1,0:T(8,128)(2,1)}), bf16[2,768,512]{2,1,0:T(8,128)(2,1)S(1)}, u32[]{:S(2)}, u32[]{:S(2)}) async-start(bf16[2,768,512]{2,1,0:T(8,128)(2,1)} %broadcast_in_dim.8), calls=%async_computation.5 | async-start | bytes 3145728 | tf_op jit(solution)/shard_map/all_to_all | solution.py:49
  206.8 21.4 %fusion.1 = f32[2,5,256,1,512]{4,3,2,1,0:T(1,128)} fusion(f32[2,5,256,3,512]{4,3,2,1,0:T(4,128)} %reshape.52), kind=kLoop, calls=%fused_computation.4 | loop fusion | flops 2621440 | bytes 31457280 | tf_op jit(solution)/shard_map/add | solution.py:131
  229.5 6.5 %fusion.2 = bf16[2,5,256,512]{3,2,1,0:T(8,128)(2,1)} fusion(f32[2,5,256,512]{3,2,1,0:T(8,128)} %bitcast.24, f32[2,5,256,1,512]{4,3,2,1,0:T(1,128)} %fusion.1), kind=kLoop, calls=%fused_computation.6 | loop fusion | flops 2621440 | bytes 13107200 | tf_op jit(solution)/shard_map/convert_element_type | solution.py:135
  (53 shorter events, 14.5 us)
Async XLA Ops:
  0.6 10.0 %copy-start = (bf16[512,18]{0,1:T(8,128)(2,1)S(1)}, bf16[512,18]{0,1:T(8,128)(2,1)}, u32[]{:S(2)}) copy-start(bf16[512,18]{0,1:T(8,128)(2,1)} %param.13) | copy-start | bytes 55300
  1.6 2.8 %copy-start.4 = (bf16[2,5,256,512]{3,2,1,0:T(8,128)(2,1)S(1)}, bf16[2,5,256,512]{3,2,1,0:T(8,128)(2,1)}, u32[]{:S(2)}) copy-start(bf16[2,5,256,512]{3,2,1,0:T(8,128)(2,1)} %param.9) | copy-start | bytes 7864324
  4.5 1.4 copy-start.6
  5.4 5.2 %copy-start.5 = (bf16[2,5,256,1536]{3,2,1,0:T(8,128)(2,1)}, bf16[2,5,256,1536]{3,2,1,0:T(8,128)(2,1)S(1)}, u32[]{:S(2)}) copy-start(bf16[2,5,256,1536]{3,2,1,0:T(8,128)(2,1)S(1)} %pad_maximum_fusion) | copy-start | bytes 23592964
  5.9 4.7 %copy-start.8 = (f32[512]{0:T(512)S(1)}, f32[512]{0:T(512)}, u32[]{:S(2)}) copy-start(f32[512]{0:T(512)} %param.12) | copy-start | bytes 6148
  5.9 4.7 %copy-start.9 = (f32[18]{0:T(128)S(1)}, f32[18]{0:T(128)}, u32[]{:S(2)}) copy-start(f32[18]{0:T(128)} %param.14) | copy-start | bytes 220
  10.6 2.3 copy-start.3
  10.6 2.3 copy-start.10
  62.3 6.4 %slice-start = ((s8[5242880]{0:T(1024)(128)(4,1)}), s8[4194304]{0:T(1024)(128)(4,1)S(1)}, s32[]{:S(2)}) async-start(s8[5242880]{0:T(1024)(128)(4,1)} %bitcast.25), calls=%async_computation.6 | async-start | bytes 8388608
  62.8 5.9 %slice-start.1 = ((s8[5242880]{0:T(1024)(128)(4,1)}), s8[1048576]{0:T(1024)(128)(4,1)S(1)}, s32[]{:S(2)}) async-start(s8[5242880]{0:T(1024)(128)(4,1)} %bitcast.25), calls=%async_computation.7 | async-start | bytes 2097152
  62.9 7.5 %slice-start.2 = ((s8[7864320]{0:T(1024)(128)(4,1)}), s8[4194304]{0:T(1024)(128)(4,1)S(1)}, s32[]{:S(2)}) async-start(s8[7864320]{0:T(1024)(128)(4,1)} %bitcast.30), calls=%async_computation.8 | async-start | bytes 8388608
  68.7 2.0 slice-start.3
  70.8 4.3 %copy-start.2 = (f32[2560,512]{1,0:T(8,128)}, f32[2560,512]{1,0:T(8,128)S(1)}, u32[]{:S(2)}) copy-start(f32[2560,512]{1,0:T(8,128)S(1)} %subtract_multiply_fusion) | copy-start | bytes 15728644
  143.1 8.1 %copy-start.7 = (bf16[1536,512]{1,0:T(8,128)(2,1)S(1)}, bf16[1536,512]{1,0:T(8,128)(2,1)}, u32[]{:S(2)}) copy-start(bf16[1536,512]{1,0:T(8,128)(2,1)} %param.11) | copy-start | bytes 4718596
  144.3 43.3 %all-to-all-start.3 = ((f32[64,6,512]{2,1,0:T(8,128)}), f32[64,6,512]{2,1,0:T(8,128)S(1)}, u32[]{:S(2)}, u32[]{:S(2)}) async-start(f32[64,6,512]{2,1,0:T(8,128)} %broadcast_in_dim.6), calls=%async_computation.3 | async-start | bytes 2097152 | tf_op jit(solution)/shard_map/all_to_all | solution.py:49
  203.1 32.8 %all-to-all-start.5 = ((bf16[2,768,512]{2,1,0:T(8,128)(2,1)}), bf16[2,768,512]{2,1,0:T(8,128)(2,1)S(1)}, u32[]{:S(2)}, u32[]{:S(2)}) async-start(bf16[2,768,512]{2,1,0:T(8,128)(2,1)} %broadcast_in_dim.8), calls=%async_computation.5 | async-start | bytes 3145728 | tf_op jit(solution)/shard_map/all_to_all | solution.py:49
  229.5 7.6 %copy-start.1 = (bf16[512,18]{0,1:T(8,128)(2,1)S(1)}, bf16[512,18]{0,1:T(8,128)(2,1)}, u32[]{:S(2)}) copy-start(bf16[512,18]{0,1:T(8,128)(2,1)} %param.13) | copy-start | bytes 55300
where the time goes:
time: 240 us; the launch traced here: 238 us
  blocking collectives  117 us (49%)
  local copies, waits for them, and re-layouts  41.5 us (17%)
  other arithmetic  38 us (16%)
  matrix products  27.8 us (12%)
  starting transfers between devices  10.6 us (4%)
  between operations  3.36 us (1%)
    psum x5, blocking collectives, one_axis_at_a_time(): shard = lax.psum(shard, axis)  47.5 us
    all_to_all x1, blocking collectives, sum_by_axis(): lax.all_to_all(nearer, far, split_axis=0, concat_axis=0, tiled=True)  36.2 us
    reshape x1, local copies, waits for them, and re-layouts, backward(): d_taps = d_taps.reshape(batch, frames, sites, 3, width)  26.1 us
    add x1, other arithmetic, backward(): padded[:, 0:frames, :, 0, :] + padded[:, 1:frames + 1, :, 1, :]  21.4 us
    all_to_all x1, blocking collectives, sum_at_owner(): tiles = lax.all_to_all(split_up(shard, dim, count), axis, 0, 0, tiled=True)  20.2 us
    all_to_all x2, starting transfers between devices, copy_for_each(): return lax.all_to_all(copies, axis, split_axis=0, concat_axis=0, tiled=True)  10.6 us
    dot_general x1, matrix products, backward(): lax.dot_general(d_conv, conv_weight, (((1,), (1,)), ((), ())), preferred_...  10.3 us
    all_to_all x1, blocking collectives, sum_at_owner_2(): tiles = lax.all_to_all(split_up(shard, dim, count), axis, 0, 0, tiled=True)  7.14 us
  transfers between devices with their start and end apart: 2, of which 0 were waited for; matrix products, arithmetic and copies ran while one was open for 27% of the time, Pallas kernels for 0%

commit v1 on v0

--- a/solution.py
+++ b/solution.py
@@ -10,7 +10,7 @@
 
 def one_axis_at_a_time(shard, axes):
     for axis in axes:
-        shard = lax.psum(shard, axis)
+        shard = jnp.sum(lax.all_gather(shard, axis), axis=0)
     return shard
 
 

time: 240 us -> 258 us (1.075)
  local copies, waits for them, and re-layouts: 41.5 us -> 56.4 us
  between operations: 3.36 us -> 6.62 us
  other arithmetic: 38 us -> 41.1 us
  blocking collectives: 117 us -> 114 us
    psum x5 -> x0, blocking collectives: 47.5 us -> none  [one_axis_at_a_time(): shard = lax.psum(shard, axis)]
    unnamed x0 -> x5, blocking collectives: none -> 44.4 us
    unnamed x31 -> x56, local copies, waits for them, and re-layouts: 3.59 us -> 18 us
    reduce_sum x0 -> x10, other arithmetic: none -> 3.11 us  [one_axis_at_a_time(): shard = jnp.sum(lax.all_gather(shard, axis), axis=0)]
  transfers between devices with their start and end apart: 2 -> 2, of which waited for: 0 -> 0; matrix products, arithmetic and copies ran while one was open for 27% -> 25% of each run, Pallas kernels for 0% -> 0%
where the time goes in v1:
time: 258 us; the launch traced here: 256 us
  blocking collectives  114 us (44%)
  local copies, waits for them, and re-layouts  56.4 us (22%)
  other arithmetic  41.1 us (16%)
  matrix products  27.8 us (11%)
  starting transfers between devices  10.6 us (4%)
  between operations  6.62 us (3%)
    unnamed x5, blocking collectives  44.4 us
    all_to_all x1, blocking collectives, sum_by_axis(): lax.all_to_all(nearer, far, split_axis=0, concat_axis=0, tiled=True)  36.2 us
    reshape x1, local copies, waits for them, and re-layouts, backward(): d_taps = d_taps.reshape(batch, frames, sites, 3, width)  26.1 us
    add x1, other arithmetic, backward(): padded[:, 0:frames, :, 0, :] + padded[:, 1:frames + 1, :, 1, :]  21.4 us
    all_to_all x1, blocking collectives, sum_at_owner(): tiles = lax.all_to_all(split_up(shard, dim, count), axis, 0, 0, tiled=True)  20.2 us
    unnamed x56, local copies, waits for them, and re-layouts  18 us
    all_to_all x2, starting transfers between devices, copy_for_each(): return lax.all_to_all(copies, axis, split_axis=0, concat_axis=0, tiled=True)  10.6 us
    dot_general x1, matrix products, backward(): lax.dot_general(d_conv, conv_weight, (((1,), (1,)), ((), ())), preferred_...  10.3 us
  transfers between devices with their start and end apart: 2, of which 0 were waited for; matrix products, arithmetic and copies ran while one was open for 25% of the time, Pallas kernels for 0%

profile of v1, /device:TPU:1, one launch (start us, length us, event | category | flops | bytes accessed | tf_op | source)
XLA Modules:
  0.0 256.3 jit_solution(8834123953920573864)
XLA Ops:
  11.3 2.7 %pad_slice_fusion.3 = (bf16[2,5,256,512]{3,2,1,0:T(8,128)(2,1)S(1)}, bf16[2,5,256,512]{3,2,1,0:T(8,128)(2,1)S(1)}) fusion(bf16[2,5,256,512]{3,2,1,0:T(8,128)(2,1)} %param.9), kind=kLoop, calls=%fused_computation.14 | loop fusion | bytes 7864320 | tf_op jit(solution)/shard_map/slice | solution.py:79
  15.6 4.6 %multiply_reduce_fusion.1 = (f32[2560]{0:T(1024)S(1)}, f32[2560,512]{1,0:T(8,128)S(1)}) fusion(bf16[2560,1536]{1,0:T(8,128)(2,1)S(1)} %bitcast.44, bf16[1536,512]{1,0:T(8,128)(2,1)S(1)} %copy-done.6, bf16[2560,512]{1,0:T(8,128)(2,1)S(1)} %bitcast.42), kind=kOutput, calls=%fused_computation.11 | convolution fusion | flops 4031772160 | bytes 17311744 | tf_op jit(solution)/shard_map/dot_general | solution.py:86
  25.4 9.3 %all-reduce.13 = (f32[72]{0:T(128)S(1)}, f32[4]{0:T(128)S(1)}) all-reduce(f32[72]{0:T(128)S(1)} %dynamic-update-slice, f32[4]{0:T(128)S(1)} %dynamic-update-slice.5), channel_id=2, replica_groups=mesh['dp_0'=4,'dp_1'=8,'dp_2'=2,'dp_3'=2,'shard'=2] {'dp_0'}, use_global_device_ids=true, to_apply=%add.2 | all-reduce | flops 76 | bytes 608
  37.0 16.2 %all-reduce.12 = (f32[144]{0:T(256)S(1)}, f32[8]{0:T(128)S(1)}) all-reduce(f32[144]{0:T(256)S(1)} %dynamic-update-slice.1, f32[8]{0:T(128)S(1)} %dynamic-update-slice.6), channel_id=3, replica_groups=mesh['dp_0'=4,'dp_1'=8,'dp_2'=2,'dp_3'=2,'shard'=2] {'dp_1'}, use_global_device_ids=true, to_apply=%add.3 | all-reduce | flops 152 | bytes 1216
  53.9 1.4 dynamic-update-slice.7
  55.6 5.3 %all-reduce.16 = (f32[36]{0:T(128)S(1)}, f32[2]{0:T(128)S(1)}) all-reduce(f32[36]{0:T(128)S(1)} %dynamic-update-slice.2, f32[2]{0:T(128)S(1)} %dynamic-update-slice.7), channel_id=4, replica_groups=mesh['dp_0'=4,'dp_1'=8,'dp_2'=2,'dp_3'=2,'shard'=2] {'dp_2'}, use_global_device_ids=true, to_apply=%add.4 | all-reduce | flops 38 | bytes 304
  63.1 9.7 %all-reduce.15 = (f32[36]{0:T(128)S(1)}, f32[2]{0:T(128)S(1)}) all-reduce(f32[36]{0:T(128)S(1)} %dynamic-update-slice.3, f32[2]{0:T(128)S(1)} %dynamic-update-slice.8), channel_id=5, replica_groups=mesh['dp_0'=4,'dp_1'=8,'dp_2'=2,'dp_3'=2,'shard'=2] {'dp_3'}, use_global_device_ids=true, to_apply=%add.5 | all-reduce | flops 38 | bytes 304
  75.1 3.9 %all-reduce.14 = (f32[36]{0:T(128)S(1)}, f32[2]{0:T(128)S(1)}) all-reduce(f32[36]{0:T(128)S(1)} %dynamic-update-slice.4, f32[2]{0:T(128)S(1)} %dynamic-update-slice.9), channel_id=6, replica_groups=mesh['dp_0'=4,'dp_1'=8,'dp_2'=2,'dp_3'=2,'shard'=2] {'shard'}, use_global_device_ids=true, to_apply=%add.6 | all-reduce | flops 38 | bytes 304
  80.3 5.8 %multiply_reduce_fusion = (f32[2560]{0:T(1024)S(1)}, f32[2560,512]{1,0:T(8,128)S(1)}) fusion(f32[2560,512]{1,0:T(8,128)} %copy-done.3, f32[2560]{0:T(1024)S(1)} %add_rsqrt_fusion, f32[512]{0:T(512)S(1)} %copy-done.8, f32[2560,18]{0,1:T(8,128)S(1)} %fusion.20, bf16[512,18]{0,1:T(8,128)(2,1)S(1)} %copy-done), kind=kOutput, calls=%fused_computation.9 | convolution fusion | flops 288355840 | bytes 10711040 | tf_op jit(solution)/shard_map/dot_general | solution.py:120
  86.2 1.6 subtract_multiply_fusion
  88.2 4.3 %convolution_convert_fusion = bf16[1536,512]{1,0:T(8,128)(2,1)S(1)} fusion(bf16[2560,1536]{1,0:T(8,128)(2,1)S(1)} %bitcast.47, f32[2560,512]{1,0:T(8,128)S(1)} %subtract_multiply_fusion), kind=kOutput, calls=%fused_computation.17 | convolution fusion | flops 4028628992 | bytes 14680064 | tf_op jit(solution)/shard_map/dot_general | solution.py:172
  92.5 20.2 %all_to_all.32 = bf16[2,768,512]{2,1,0:T(8,128)(2,1)S(1)} all-to-all(bf16[2,768,512]{2,1,0:T(8,128)(2,1)S(1)} %bitcast.50), channel_id=1, replica_groups=mesh['dp_0'=4,'dp_1'=8,'dp_2'=2,'dp_3'=2,'shard'=2] {'shard'}, dimensions={0} | all-to-all | bytes 3145728 | tf_op jit(solution)/shard_map/all_to_all | solution.py:24
  112.7 1.5 convert_reduce_fusion
  114.2 1.5 reshape_reshape.6
  116.6 7.1 %all_to_all.30 = f32[2,64,6,512]{3,1,2,0:T(8,128)S(1)} all-to-all(f32[2,64,6,512]{3,1,2,0:T(8,128)S(1)} %copy.31), channel_id=1, replica_groups=mesh['dp_0'=4,'dp_1'=8,'dp_2'=2,'dp_3'=2,'shard'=2] {'dp_3'}, dimensions={0} | all-to-all | bytes 3145728 | tf_op jit(solution)/shard_map/all_to_all | solution.py:30
  124.4 36.2 %all_to_all.33 = f32[64,6,512]{2,1,0:T(8,128)S(1)} all-to-all(f32[64,6,512]{2,1,0:T(8,128)S(1)} %copy.32), channel_id=1, replica_groups=mesh['dp_0'=4,'dp_1'=8,'dp_2'=2,'dp_3'=2,'shard'=2] {'dp_0','dp_1','dp_2'}, dimensions={0} | all-to-all | bytes 1572864 | tf_op jit(solution)/shard_map/all_to_all | solution.py:38
  161.8 6.9 %all-to-all-start.3 = ((f32[64,6,512]{2,1,0:T(8,128)}), f32[64,6,512]{2,1,0:T(8,128)S(1)}, u32[]{:S(2)}, u32[]{:S(2)}) async-start(f32[64,6,512]{2,1,0:T(8,128)} %broadcast_in_dim.6), calls=%async_computation.3 | async-start | bytes 2097152 | tf_op jit(solution)/shard_map/all_to_all | solution.py:49
  168.7 10.3 %fusion.6 = f32[2560,1536]{1,0:T(8,128)} fusion(bf16[1536,512]{1,0:T(8,128)(2,1)S(1)} %copy-done.7, f32[2560,512]{1,0:T(8,128)} %copy-done.2), kind=kOutput, calls=%fused_computation.24 | convolution fusion | flops 4027842560 | bytes 22544384 | tf_op jit(solution)/shard_map/dot_general | solution.py:125
  179.0 26.1 %reshape.57 = f32[2,5,256,3,512]{4,3,2,1,0:T(4,128)} reshape(f32[2560,1536]{1,0:T(8,128)} %fusion.6) | data formatting | bytes 31457280 | tf_op jit(solution)/shard_map/reshape | solution.py:128
  205.7 6.0 %all_to_all.31 = f32[2,64,6,512]{3,1,2,0:T(8,128)S(1)} all-to-all(f32[2,64,6,512]{3,1,2,0:T(8,128)S(1)} %broadcast_in_dim.7), channel_id=1, replica_groups=mesh['dp_0'=4,'dp_1'=8,'dp_2'=2,'dp_3'=2,'shard'=2] {'dp_3'}, dimensions={0} | all-to-all | bytes 3145728 | tf_op jit(solution)/shard_map/all_to_all | solution.py:49
  214.0 5.3 %subtract_convert_fusion = (bf16[768,512]{1,0:T(8,128)(2,1)S(1)}, f32[768,512]{1,0:T(8,128)}, f32[768,512]{1,0:T(8,128)}) fusion(bf16[1536,512]{1,0:T(8,128)(2,1)} %param.11, s32[]{:T(128)S(6)} %select_n.7, f32[768,512]{1,0:T(8,128)} %reshape_reshape.7, f32[768,512]{1,0:T(8,128)} %param.16, f32[768,512]{1,0:T(8,128)} %param.17), kind=kLoop, calls=%fused_computation.22 | loop fusion | flops 5111808 | bytes 9437188 | tf_op jit(solution)/shard_map/convert_element_type | solution.py:185
  220.6 3.7 %all-to-all-start.5 = ((bf16[2,768,512]{2,1,0:T(8,128)(2,1)}), bf16[2,768,512]{2,1,0:T(8,128)(2,1)S(1)}, u32[]{:S(2)}, u32[]{:S(2)}) async-start(bf16[2,768,512]{2,1,0:T(8,128)(2,1)} %broadcast_in_dim.8), calls=%async_computation.5 | async-start | bytes 3145728 | tf_op jit(solution)/shard_map/all_to_all | solution.py:49
  224.2 21.4 %fusion.1 = f32[2,5,256,1,512]{4,3,2,1,0:T(1,128)} fusion(f32[2,5,256,3,512]{4,3,2,1,0:T(4,128)} %reshape.57), kind=kLoop, calls=%fused_computation.4 | loop fusion | flops 2621440 | bytes 31457280 | tf_op jit(solution)/shard_map/add | solution.py:131
  247.5 6.5 %fusion.2 = bf16[2,5,256,512]{3,2,1,0:T(8,128)(2,1)} fusion(f32[2,5,256,512]{3,2,1,0:T(8,128)} %bitcast.39, f32[2,5,256,1,512]{4,3,2,1,0:T(1,128)} %fusion.1), kind=kLoop, calls=%fused_computation.6 | loop fusion | flops 2621440 | bytes 13107200 | tf_op jit(solution)/shard_map/convert_element_type | solution.py:135
  (93 shorter events, 32.4 us)
Async XLA Ops:
  0.6 19.6 %copy-start = (bf16[512,18]{0,1:T(8,128)(2,1)S(1)}, bf16[512,18]{0,1:T(8,128)(2,1)}, u32[]{:S(2)}) copy-start(bf16[512,18]{0,1:T(8,128)(2,1)} %param.13) | copy-start | bytes 55300
  11.3 2.8 %copy-start.4 = (bf16[2,5,256,512]{3,2,1,0:T(8,128)(2,1)S(1)}, bf16[2,5,256,512]{3,2,1,0:T(8,128)(2,1)}, u32[]{:S(2)}) copy-start(bf16[2,5,256,512]{3,2,1,0:T(8,128)(2,1)} %param.9) | copy-start | bytes 7864324
  14.2 1.4 copy-start.6
  15.0 5.2 %copy-start.5 = (bf16[2,5,256,1536]{3,2,1,0:T(8,128)(2,1)}, bf16[2,5,256,1536]{3,2,1,0:T(8,128)(2,1)S(1)}, u32[]{:S(2)}) copy-start(bf16[2,5,256,1536]{3,2,1,0:T(8,128)(2,1)S(1)} %pad_maximum_fusion) | copy-start | bytes 23592964
  15.6 4.7 %copy-start.8 = (f32[512]{0:T(512)S(1)}, f32[512]{0:T(512)}, u32[]{:S(2)}) copy-start(f32[512]{0:T(512)} %param.12) | copy-start | bytes 6148
  15.6 4.7 %copy-start.9 = (f32[18]{0:T(128)S(1)}, f32[18]{0:T(128)}, u32[]{:S(2)}) copy-start(f32[18]{0:T(128)} %param.14) | copy-start | bytes 220
  20.2 2.3 copy-start.3
  20.3 2.3 copy-start.10
  79.8 6.4 %slice-start = ((s8[5242880]{0:T(1024)(128)(4,1)}), s8[4194304]{0:T(1024)(128)(4,1)S(1)}, s32[]{:S(2)}) async-start(s8[5242880]{0:T(1024)(128)(4,1)} %bitcast.40), calls=%async_computation.6 | async-start | bytes 8388608
  80.3 5.9 %slice-start.1 = ((s8[5242880]{0:T(1024)(128)(4,1)}), s8[1048576]{0:T(1024)(128)(4,1)S(1)}, s32[]{:S(2)}) async-start(s8[5242880]{0:T(1024)(128)(4,1)} %bitcast.40), calls=%async_computation.7 | async-start | bytes 2097152
  80.3 7.5 %slice-start.2 = ((s8[7864320]{0:T(1024)(128)(4,1)}), s8[4194304]{0:T(1024)(128)(4,1)S(1)}, s32[]{:S(2)}) async-start(s8[7864320]{0:T(1024)(128)(4,1)} %bitcast.45), calls=%async_computation.8 | async-start | bytes 8388608
  86.2 2.0 slice-start.3
  88.2 4.3 %copy-start.2 = (f32[2560,512]{1,0:T(8,128)}, f32[2560,512]{1,0:T(8,128)S(1)}, u32[]{:S(2)}) copy-start(f32[2560,512]{1,0:T(8,128)S(1)} %subtract_multiply_fusion) | copy-start | bytes 15728644
  160.6 8.1 %copy-start.7 = (bf16[1536,512]{1,0:T(8,128)(2,1)S(1)}, bf16[1536,512]{1,0:T(8,128)(2,1)}, u32[]{:S(2)}) copy-start(bf16[1536,512]{1,0:T(8,128)(2,1)} %param.11) | copy-start | bytes 4718596
  161.8 43.3 %all-to-all-start.3 = ((f32[64,6,512]{2,1,0:T(8,128)}), f32[64,6,512]{2,1,0:T(8,128)S(1)}, u32[]{:S(2)}, u32[]{:S(2)}) async-start(f32[64,6,512]{2,1,0:T(8,128)} %broadcast_in_dim.6), calls=%async_computation.3 | async-start | bytes 2097152 | tf_op jit(solution)/shard_map/all_to_all | solution.py:49
  220.6 33.4 %all-to-all-start.5 = ((bf16[2,768,512]{2,1,0:T(8,128)(2,1)}), bf16[2,768,512]{2,1,0:T(8,128)(2,1)S(1)}, u32[]{:S(2)}, u32[]{:S(2)}) async-start(bf16[2,768,512]{2,1,0:T(8,128)(2,1)} %broadcast_in_dim.8), calls=%async_computation.5 | async-start | bytes 3145728 | tf_op jit(solution)/shard_map/all_to_all | solution.py:49
  247.5 7.6 %copy-start.1 = (bf16[512,18]{0,1:T(8,128)(2,1)S(1)}, bf16[512,18]{0,1:T(8,128)(2,1)}, u32[]{:S(2)}) copy-start(bf16[512,18]{0,1:T(8,128)(2,1)} %param.13) | copy-start | bytes 55300
